TPU v7x, 768 devices: a whole 4x8x12 slice. The times are simulated.
768 devices in a mesh: blk: 96 (over x, y, z_lo), uly: 8 (over z_hi, core).
Axes of the slice: x: 4, y: 8, z: 12 (z_hi: 4, z_lo: 3; z = z_hi * 3 + z_lo), core: 2. Of those that a mesh axis runs over, the one named last changes fastest.
Arguments:
- stored_query_rows: bfloat16 [12288, 5120], P('blk', 'uly'), may hold values from -4 to 4
- key_states: bfloat16 [12288, 1024], P('blk', 'uly'), may hold values from -4 to 4
- value_states: bfloat16 [12288, 1024], P('blk', 'uly'), may hold values from -6 to 6
- attn_output: bfloat16 [12288, 5120], P('blk', 'uly'), may hold values from -6 to 6
- output_grad: bfloat16 [12288, 5120], P(('blk', 'uly')), may hold values from -48 to 48
- logsumexp: float32 [40, 12288], P('uly', 'blk'), may hold values from 7 to 8.5
Outputs:
- query_gradient: bfloat16 [12288, 5120], P(('blk', 'uly'))
- key_grad: bfloat16 [12288, 1024], P(('blk', 'uly'))
- value_grad: bfloat16 [12288, 1024], P(('blk', 'uly'))
All inputs are finite; a program needn't handle non-finite values.
Results may differ from a plain program's by a relative error of at most 0.0055.
Values may be sent and summed in bfloat16 or wider, within the bound.
A program may use at most 32 MiB of HBM per device.

v0:
```python
import jax
import jax.numpy as jnp
from jax import lax
from jax.sharding import PartitionSpec as P

QHEADS = 40
KVHEADS = 8
HEAD_DIM = 128
STEPS = 3


def shifted(array, axis, by):
    size = lax.axis_size(axis)
    return lax.ppermute(array, axis, [(i, (i + by) % size) for i in range(size)])


def block_grads(
    query_heads, gradient_per_head, lse_heads, delta_per_head, key_block, value_block, score_scale
):
    scores = jnp.einsum(
        "tgrd,ugd->grtu", query_heads, key_block, preferred_element_type=jnp.float32
    )
    prob_tile = jnp.exp(scores * score_scale - lse_heads[..., None])
    grad_probs = jnp.einsum(
        "tgrd,ugd->grtu", gradient_per_head, value_block, preferred_element_type=jnp.float32
    )
    grad_scores = (prob_tile * (grad_probs - delta_per_head[..., None])).astype(jnp.bfloat16)
    prob_low = prob_tile.astype(jnp.bfloat16)
    value_part = jnp.einsum(
        "grtu,tgrd->ugd", prob_low, gradient_per_head, preferred_element_type=jnp.float32
    )
    query_part = jnp.einsum(
        "grtu,ugd->tgrd", grad_scores, key_block, preferred_element_type=jnp.float32
    )
    key_portion = jnp.einsum(
        "grtu,tgrd->ugd", grad_scores, query_heads, preferred_element_type=jnp.float32
    )
    return (query_part, key_portion, value_part)


def body(stored_query_rows, key_states, value_states, attn_output, output_grad, logsumexp):
    group_size = QHEADS // KVHEADS
    score_scale = HEAD_DIM ** (-0.5)
    block_rows = stored_query_rows.shape[0]
    kv_local = key_states.shape[1] // HEAD_DIM
    head_shape = (block_rows, kv_local, group_size, HEAD_DIM)
    key_shape = (block_rows, kv_local, HEAD_DIM)
    flattened_shape = (block_rows, kv_local * HEAD_DIM)
    grad_local = lax.all_to_all(output_grad, "uly", split_axis=1, concat_axis=0, tiled=True)
    query_heads = stored_query_rows.reshape(head_shape)
    gradient_per_head = grad_local.reshape(head_shape)
    output_per_head = attn_output.reshape(head_shape)
    delta_per_head = jnp.einsum(
        "lpnc,lpnc->pnl", gradient_per_head, output_per_head, preferred_element_type=jnp.float32
    )
    lse_heads = logsumexp.reshape(kv_local, group_size, block_rows)

    def tile_grads(key_block, value_block):
        return block_grads(
            query_heads,
            gradient_per_head,
            lse_heads,
            delta_per_head,
            key_block.reshape(key_shape),
            value_block.reshape(key_shape),
            score_scale,
        )

    query_sum, key_own, value_own = tile_grads(key_states, value_states)
    key_sum = key_own.reshape(flattened_shape)
    value_sum = value_own.reshape(flattened_shape)
    for offset in range(1, STEPS):
        far_key, far_value = shifted((key_states, value_states), "blk", offset)
        query_part, key_portion, value_part = tile_grads(far_key, far_value)
        query_sum = query_sum + query_part
        home_key, home_value = shifted(
            (key_portion.reshape(flattened_shape), value_part.reshape(flattened_shape)),
            "blk",
            -offset,
        )
        key_sum = key_sum + home_key
        value_sum = value_sum + home_value
    query_low = (score_scale * query_sum).astype(jnp.bfloat16).reshape(block_rows, -1)
    key_low = (score_scale * key_sum).astype(jnp.bfloat16)
    value_low = value_sum.astype(jnp.bfloat16)
    query_gradient, key_grad, value_grad = (
        lax.all_to_all(query_low, "uly", split_axis=0, concat_axis=1, tiled=True),
        lax.all_to_all(key_low, "uly", split_axis=0, concat_axis=1, tiled=True),
        lax.all_to_all(value_low, "uly", split_axis=0, concat_axis=1, tiled=True),
    )
    return (query_gradient, key_grad, value_grad)


def solution(mesh):
    placed = (
        P("blk", "uly"),
        P("blk", "uly"),
        P("blk", "uly"),
        P("blk", "uly"),
        P(("blk", "uly"), None),
        P("uly", "blk"),
    )
    return jax.shard_map(
        body,
        mesh=mesh,
        in_specs=placed,
        out_specs=(P(("blk", "uly"), None), P(("blk", "uly"), None), P(("blk", "uly"), None)),
        check_vma=False,
    )
```

profile of v0, /device:TPU:1, one launch (start us, length us, event | category | flops | bytes accessed | tf_op | source)
XLA Modules:
  0.0 113.0 jit_solution(6357512046292485495)
XLA Ops:
  0.6 6.6 %collective-permute-start.3 = (bf16[128,128]{1,0:T(8,128)(2,1)}, bf16[128,128]{1,0:T(8,128)(2,1)S(1)}, u32[]{:S(2)}, u32[]{:S(2)}) collective-permute-start(bf16[128,128]{1,0:T(8,128)(2,1)} %param.8), channel_id=1, source_target_pairs={{0,16},{8,24},{16,32},{24,40},{32,48},{40,56},{48,64},{56,72},{64,... | collective-permute-start | bytes 98312 | tf_op jit(solution)/shard_map/ppermute | solution.py:14
  7.3 1.9 %collective-permute-start.1 = (bf16[128,128]{1,0:T(8,128)(2,1)}, bf16[128,128]{1,0:T(8,128)(2,1)S(1)}, u32[]{:S(2)}, u32[]{:S(2)}) collective-permute-start(bf16[128,128]{1,0:T(8,128)(2,1)} %param.8), channel_id=1, source_target_pairs={{0,8},{8,16},{16,24},{24,32},{32,40},{40,48},{48,56},{56,64},{64,7... | collective-permute-start | bytes 98312 | tf_op jit(solution)/shard_map/ppermute | solution.py:14
  9.2 5.3 %collective-permute-start.2 = (bf16[128,128]{1,0:T(8,128)(2,1)}, bf16[128,128]{1,0:T(8,128)(2,1)S(1)}, u32[]{:S(2)}, u32[]{:S(2)}) collective-permute-start(bf16[128,128]{1,0:T(8,128)(2,1)} %param.7), channel_id=1, source_target_pairs={{0,16},{8,24},{16,32},{24,40},{32,48},{40,56},{48,64},{56,72},{64,... | collective-permute-start | bytes 98312 | tf_op jit(solution)/shard_map/ppermute | solution.py:14
  14.5 1.9 %collective-permute-start = (bf16[128,128]{1,0:T(8,128)(2,1)}, bf16[128,128]{1,0:T(8,128)(2,1)S(1)}, u32[]{:S(2)}, u32[]{:S(2)}) collective-permute-start(bf16[128,128]{1,0:T(8,128)(2,1)} %param.7), channel_id=1, source_target_pairs={{0,8},{8,16},{16,24},{24,32},{32,40},{40,48},{48,56},{56,64},{64,7... | collective-permute-start | bytes 98312 | tf_op jit(solution)/shard_map/ppermute | solution.py:14
  16.4 1.6 %copy.86 = bf16[2,8,8,640]{3,2,0,1:T(8,128)(2,1)} copy(bf16[2,8,8,640]{3,2,1,0:T(8,128)(2,1)} %bitcast.189) | data formatting | bytes 327680 | tf_op jit(solution)/shard_map/all_to_all | solution.py:49
  18.0 16.2 %all-to-all-start = ((bf16[16,8,640]{2,0,1:T(8,128)(2,1)}), bf16[16,8,640]{2,0,1:T(8,128)(2,1)S(1)}, u32[]{:S(2)}, u32[]{:S(2)}) async-start(bf16[16,8,640]{2,0,1:T(8,128)(2,1)} %bitcast.179), calls=%async_computation | async-start | bytes 327680 | tf_op jit(solution)/shard_map/all_to_all | solution.py:49
  34.4 0.6 copy-done.2
  35.1 0.7 copy-done.1
  36.5 8.3 %all-to-all-done = bf16[16,8,640]{2,0,1:T(8,128)(2,1)S(1)} async-done(((bf16[16,8,640]{2,0,1:T(8,128)(2,1)}), bf16[16,8,640]{2,0,1:T(8,128)(2,1)S(1)}, u32[]{:S(2)}, u32[]{:S(2)}) %all-to-all-start) | async-done | bytes 163872 | tf_op jit(solution)/shard_map/all_to_all | solution.py:49
  45.5 0.2 fusion.23
  45.9 6.4 %collective-permute-start.5 = (f32[128,128]{1,0:T(8,128)S(1)}, f32[128,128]{1,0:T(8,128)S(1)}, u32[]{:S(2)}, u32[]{:S(2)}) collective-permute-start(f32[128,128]{1,0:T(8,128)S(1)} %convolution_bitcast_fusion.6), channel_id=1, source_target_pairs={{0,752},{8,760},{16,0},{24,8},{32,16},{40,24},{48,32},{56,40},{64,... | collective-permute-start | bytes 196616 | tf_op jit(solution)/shard_map/ppermute | solution.py:14
  52.3 6.1 %collective-permute-start.7 = (f32[128,128]{1,0:T(8,128)S(1)}, f32[128,128]{1,0:T(8,128)S(1)}, u32[]{:S(2)}, u32[]{:S(2)}) collective-permute-start(f32[128,128]{1,0:T(8,128)S(1)} %convolution_bitcast_fusion.3), channel_id=1, source_target_pairs={{0,752},{8,760},{16,0},{24,8},{32,16},{40,24},{48,32},{56,40},{64,... | collective-permute-start | bytes 196616 | tf_op jit(solution)/shard_map/ppermute | solution.py:14
  58.6 0.2 fusion.22
  59.0 1.9 %collective-permute-start.4 = (f32[128,128]{1,0:T(8,128)S(1)}, f32[128,128]{1,0:T(8,128)S(1)}, u32[]{:S(2)}, u32[]{:S(2)}) collective-permute-start(f32[128,128]{1,0:T(8,128)S(1)} %convolution_bitcast_fusion.7), channel_id=1, source_target_pairs={{0,760},{8,0},{16,8},{24,16},{32,24},{40,32},{48,40},{56,48},{64,5... | collective-permute-start | bytes 196616 | tf_op jit(solution)/shard_map/ppermute | solution.py:14
  61.0 3.1 %collective-permute-start.6 = (f32[128,128]{1,0:T(8,128)S(1)}, f32[128,128]{1,0:T(8,128)S(1)}, u32[]{:S(2)}, u32[]{:S(2)}) collective-permute-start(f32[128,128]{1,0:T(8,128)S(1)} %convolution_bitcast_fusion.4), channel_id=1, source_target_pairs={{0,760},{8,0},{16,8},{24,16},{32,24},{40,32},{48,40},{56,48},{64,5... | collective-permute-start | bytes 196616 | tf_op jit(solution)/shard_map/ppermute | solution.py:14
  64.1 0.2 fusion.21
  64.3 0.2 fusion.44
  64.5 0.2 convolution_add_fusion.1
  64.8 1.2 %collective-permute-done.6 = f32[128,128]{1,0:T(8,128)S(1)} collective-permute-done((f32[128,128]{1,0:T(8,128)S(1)}, f32[128,128]{1,0:T(8,128)S(1)}, u32[]{:S(2)}, u32[]{:S(2)}) %collective-permute-start.6) | collective-permute-done | bytes 65568 | tf_op jit(solution)/shard_map/ppermute | solution.py:14
  66.0 0.8 fusion.29
  66.8 7.1 %all-to-all-start.3 = ((bf16[8,16,128]{2,1,0:T(8,128)(2,1)}), bf16[8,16,128]{2,1,0:T(8,128)(2,1)S(1)}, u32[]{:S(2)}, u32[]{:S(2)}) async-start(bf16[8,16,128]{2,1,0:T(8,128)(2,1)} %bitcast.43), calls=%async_computation.3 | async-start | bytes 65536 | tf_op jit(solution)/shard_map/all_to_all | solution.py:89
  73.9 0.8 fusion.30
  74.7 8.7 %all-to-all-done.3 = bf16[8,16,128]{2,1,0:T(8,128)(2,1)S(1)} async-done(((bf16[8,16,128]{2,1,0:T(8,128)(2,1)}), bf16[8,16,128]{2,1,0:T(8,128)(2,1)S(1)}, u32[]{:S(2)}, u32[]{:S(2)}) %all-to-all-start.3) | async-done | bytes 32800 | tf_op jit(solution)/shard_map/all_to_all | solution.py:89
  83.4 4.4 %all-to-all-start.2 = ((bf16[8,16,128]{2,1,0:T(8,128)(2,1)}), bf16[8,16,128]{2,1,0:T(8,128)(2,1)S(1)}, u32[]{:S(2)}, u32[]{:S(2)}) async-start(bf16[8,16,128]{2,1,0:T(8,128)(2,1)} %bitcast.35), calls=%async_computation.2 | async-start | bytes 65536 | tf_op jit(solution)/shard_map/all_to_all | solution.py:88
  87.8 0.2 fusion.20
  88.2 0.9 all_to_all.57
  89.1 8.6 %all-to-all-done.2 = bf16[8,16,128]{2,1,0:T(8,128)(2,1)S(1)} async-done(((bf16[8,16,128]{2,1,0:T(8,128)(2,1)}), bf16[8,16,128]{2,1,0:T(8,128)(2,1)S(1)}, u32[]{:S(2)}, u32[]{:S(2)}) %all-to-all-start.2) | async-done | bytes 32800 | tf_op jit(solution)/shard_map/all_to_all | solution.py:88
  97.6 4.0 %all-to-all-start.1 = ((bf16[8,16,640]{2,1,0:T(8,128)(2,1)}), bf16[8,16,640]{2,1,0:T(8,128)(2,1)S(1)}, u32[]{:S(2)}, u32[]{:S(2)}) async-start(bf16[8,16,640]{2,1,0:T(8,128)(2,1)} %all_to_all.57), calls=%async_computation.1 | async-start | bytes 327680 | tf_op jit(solution)/shard_map/all_to_all | solution.py:87
  101.7 0.6 copy_bitcast_fusion.1
  102.3 0.6 copy_bitcast_fusion.2
  102.9 9.4 %all-to-all-done.1 = bf16[8,16,640]{2,1,0:T(8,128)(2,1)S(1)} async-done(((bf16[8,16,640]{2,1,0:T(8,128)(2,1)}), bf16[8,16,640]{2,1,0:T(8,128)(2,1)S(1)}, u32[]{:S(2)}, u32[]{:S(2)}) %all-to-all-start.1) | async-done | bytes 163872 | tf_op jit(solution)/shard_map/all_to_all | solution.py:87
  112.3 0.7 copy.80
  (30 shorter events, 2.3 us)
Async XLA Ops:
  0.6 44.9 %collective-permute-start.3 = (bf16[128,128]{1,0:T(8,128)(2,1)}, bf16[128,128]{1,0:T(8,128)(2,1)S(1)}, u32[]{:S(2)}, u32[]{:S(2)}) collective-permute-start(bf16[128,128]{1,0:T(8,128)(2,1)} %param.8), channel_id=1, source_target_pairs={{0,16},{8,24},{16,32},{24,40},{32,48},{40,56},{48,64},{56,72},{64,... | collective-permute-start | bytes 98312 | tf_op jit(solution)/shard_map/ppermute | solution.py:14
  7.3 51.3 %collective-permute-start.1 = (bf16[128,128]{1,0:T(8,128)(2,1)}, bf16[128,128]{1,0:T(8,128)(2,1)S(1)}, u32[]{:S(2)}, u32[]{:S(2)}) collective-permute-start(bf16[128,128]{1,0:T(8,128)(2,1)} %param.8), channel_id=1, source_target_pairs={{0,8},{8,16},{16,24},{24,32},{32,40},{40,48},{48,56},{56,64},{64,7... | collective-permute-start | bytes 98312 | tf_op jit(solution)/shard_map/ppermute | solution.py:14
  9.2 26.8 %collective-permute-start.2 = (bf16[128,128]{1,0:T(8,128)(2,1)}, bf16[128,128]{1,0:T(8,128)(2,1)S(1)}, u32[]{:S(2)}, u32[]{:S(2)}) collective-permute-start(bf16[128,128]{1,0:T(8,128)(2,1)} %param.7), channel_id=1, source_target_pairs={{0,16},{8,24},{16,32},{24,40},{32,48},{40,56},{48,64},{56,72},{64,... | collective-permute-start | bytes 98312 | tf_op jit(solution)/shard_map/ppermute | solution.py:14
  14.5 21.8 %collective-permute-start = (bf16[128,128]{1,0:T(8,128)(2,1)}, bf16[128,128]{1,0:T(8,128)(2,1)S(1)}, u32[]{:S(2)}, u32[]{:S(2)}) collective-permute-start(bf16[128,128]{1,0:T(8,128)(2,1)} %param.7), channel_id=1, source_target_pairs={{0,8},{8,16},{16,24},{24,32},{32,40},{40,48},{48,56},{56,64},{64,7... | collective-permute-start | bytes 98312 | tf_op jit(solution)/shard_map/ppermute | solution.py:14
  18.0 16.2 %copy-start = (bf16[128,640]{1,0:T(8,128)(2,1)S(1)}, bf16[128,640]{1,0:T(8,128)(2,1)}, u32[]{:S(2)}) copy-start(bf16[128,640]{1,0:T(8,128)(2,1)} %param.6) | copy-start | bytes 491524
  18.0 26.8 %all-to-all-start = ((bf16[16,8,640]{2,0,1:T(8,128)(2,1)}), bf16[16,8,640]{2,0,1:T(8,128)(2,1)S(1)}, u32[]{:S(2)}, u32[]{:S(2)}) async-start(bf16[16,8,640]{2,0,1:T(8,128)(2,1)} %bitcast.179), calls=%async_computation | async-start | bytes 327680 | tf_op jit(solution)/shard_map/all_to_all | solution.py:49
  34.2 0.8 copy-start.2
  34.2 0.8 copy-start.3
  34.9 0.9 copy-start.1
  45.9 28.0 %collective-permute-start.5 = (f32[128,128]{1,0:T(8,128)S(1)}, f32[128,128]{1,0:T(8,128)S(1)}, u32[]{:S(2)}, u32[]{:S(2)}) collective-permute-start(f32[128,128]{1,0:T(8,128)S(1)} %convolution_bitcast_fusion.6), channel_id=1, source_target_pairs={{0,752},{8,760},{16,0},{24,8},{32,16},{40,24},{48,32},{56,40},{64,... | collective-permute-start | bytes 196616 | tf_op jit(solution)/shard_map/ppermute | solution.py:14
  52.3 12.4 %collective-permute-start.7 = (f32[128,128]{1,0:T(8,128)S(1)}, f32[128,128]{1,0:T(8,128)S(1)}, u32[]{:S(2)}, u32[]{:S(2)}) collective-permute-start(f32[128,128]{1,0:T(8,128)S(1)} %convolution_bitcast_fusion.3), channel_id=1, source_target_pairs={{0,752},{8,760},{16,0},{24,8},{32,16},{40,24},{48,32},{56,40},{64,... | collective-permute-start | bytes 196616 | tf_op jit(solution)/shard_map/ppermute | solution.py:14
  58.8 5.2 %copy-start.4 = (bf16[128,128]{1,0:T(8,128)(2,1)S(1)}, bf16[128,128]{1,0:T(8,128)(2,1)}, u32[]{:S(2)}) copy-start(bf16[128,128]{1,0:T(8,128)(2,1)} %param.8) | copy-start | bytes 98308
  59.0 14.8 %collective-permute-start.4 = (f32[128,128]{1,0:T(8,128)S(1)}, f32[128,128]{1,0:T(8,128)S(1)}, u32[]{:S(2)}, u32[]{:S(2)}) collective-permute-start(f32[128,128]{1,0:T(8,128)S(1)} %convolution_bitcast_fusion.7), channel_id=1, source_target_pairs={{0,760},{8,0},{16,8},{24,16},{32,24},{40,32},{48,40},{56,48},{64,5... | collective-permute-start | bytes 196616 | tf_op jit(solution)/shard_map/ppermute | solution.py:14
  61.0 5.0 %collective-permute-start.6 = (f32[128,128]{1,0:T(8,128)S(1)}, f32[128,128]{1,0:T(8,128)S(1)}, u32[]{:S(2)}, u32[]{:S(2)}) collective-permute-start(f32[128,128]{1,0:T(8,128)S(1)} %convolution_bitcast_fusion.4), channel_id=1, source_target_pairs={{0,760},{8,0},{16,8},{24,16},{32,24},{40,32},{48,40},{56,48},{64,5... | collective-permute-start | bytes 196616 | tf_op jit(solution)/shard_map/ppermute | solution.py:14
  66.8 16.6 %all-to-all-start.3 = ((bf16[8,16,128]{2,1,0:T(8,128)(2,1)}), bf16[8,16,128]{2,1,0:T(8,128)(2,1)S(1)}, u32[]{:S(2)}, u32[]{:S(2)}) async-start(bf16[8,16,128]{2,1,0:T(8,128)(2,1)} %bitcast.43), calls=%async_computation.3 | async-start | bytes 65536 | tf_op jit(solution)/shard_map/all_to_all | solution.py:89
  83.4 14.2 %all-to-all-start.2 = ((bf16[8,16,128]{2,1,0:T(8,128)(2,1)}), bf16[8,16,128]{2,1,0:T(8,128)(2,1)S(1)}, u32[]{:S(2)}, u32[]{:S(2)}) async-start(bf16[8,16,128]{2,1,0:T(8,128)(2,1)} %bitcast.35), calls=%async_computation.2 | async-start | bytes 65536 | tf_op jit(solution)/shard_map/all_to_all | solution.py:88
  97.6 14.7 %all-to-all-start.1 = ((bf16[8,16,640]{2,1,0:T(8,128)(2,1)}), bf16[8,16,640]{2,1,0:T(8,128)(2,1)S(1)}, u32[]{:S(2)}, u32[]{:S(2)}) async-start(bf16[8,16,640]{2,1,0:T(8,128)(2,1)} %all_to_all.57), calls=%async_computation.1 | async-start | bytes 327680 | tf_op jit(solution)/shard_map/all_to_all | solution.py:87
where the time goes:
time: 114 us; the launch traced here: 113 us
  starting transfers between devices  64.9 us (57%)
  waiting for transfers between devices  36.2 us (32%)
  local copies, waits for them, and re-layouts  6.55 us (6%)
  matrix products  4.34 us (4%)
    ppermute x8, starting transfers between devices, shifted(): lax.ppermute(array, axis, [(i, (i + by) % size) for i in range(size)])  33.2 us
    all_to_all x1, starting transfers between devices, body(): lax.all_to_all(output_grad, 'uly', split_axis=1, concat_axis=0, tiled=True)  16.2 us
    all_to_all x1, waiting for transfers between devices, body(): lax.all_to_all(query_low, 'uly', split_axis=0, concat_axis=1, tiled=True)  9.4 us
    all_to_all x1, waiting for transfers between devices, body(): lax.all_to_all(value_low, 'uly', split_axis=0, concat_axis=1, tiled=True)  8.71 us
    all_to_all x1, waiting for transfers between devices, body(): lax.all_to_all(key_low, 'uly', split_axis=0, concat_axis=1, tiled=True)  8.58 us
    all_to_all x1, waiting for transfers between devices, body(): lax.all_to_all(output_grad, 'uly', split_axis=1, concat_axis=0, tiled=True)  8.34 us
    all_to_all x1, starting transfers between devices, body(): lax.all_to_all(value_low, 'uly', split_axis=0, concat_axis=1, tiled=True)  7.09 us
    all_to_all x1, starting transfers between devices, body(): lax.all_to_all(key_low, 'uly', split_axis=0, concat_axis=1, tiled=True)  4.39 us
  transfers between devices with their start and end apart: 12, of which 5 were waited for; matrix products, arithmetic and copies ran while one was open for 7% of the time, Pallas kernels for 0%

commit v1 on v0

v1 whole, which is shorter than its diff:
```python
import jax
import jax.numpy as jnp
from jax import lax
from jax.experimental import pallas as pl
from jax.experimental.pallas import tpu as pltpu
from jax.sharding import PartitionSpec as P

QHEADS = 40
KVHEADS = 8
HEAD_DIM = 128
STEPS = 3
MESH = pl.DeviceIdType.MESH
F32 = jnp.float32
BF16 = jnp.bfloat16

HOPS = ((2, 0), (2, 1), (1, 0), (3, 0), (1, 1), (3, 1), (0, 1))


def dot_nt(a, b):
    return lax.dot_general(a, b, (((1,), (1,)), ((), ())), preferred_element_type=F32)


def dot_nn(a, b):
    return lax.dot_general(a, b, (((1,), (0,)), ((), ())), preferred_element_type=F32)


def kernel(
    blocks, ulys,
    q_hbm, k_hbm, v_hbm, o_hbm, g_hbm, lse_hbm,
    dq_out, dk_out, dv_out,
    q, k, v, o, g, lse, kt, prob, prob_low, dscore, delta, own, part, far, dq, final,
    local_sem, local_out_sem, g_send, g_recv, kv_send, kv_recv, p_send, p_recv,
    dq_send, dq_recv, f_send, f_recv,
):
    group = q.shape[1] // HEAD_DIM
    tokens = q.shape[0]
    piece = tokens // ulys
    width = q.shape[1]
    scale = HEAD_DIM ** -0.5
    b = lax.axis_index("blk")
    u = lax.axis_index("uly")
    chips = ulys // 2
    zc = u // 2
    core = u % 2

    def peer(hop):
        return ((zc + hop[0]) % chips) * 2 + (core + hop[1]) % 2

    peers = [peer(hop) for hop in HOPS]
    later = [(b + i) % blocks for i in range(STEPS)]
    earlier = [(b + blocks - i) % blocks for i in range(STEPS)]

    barrier = pltpu.get_barrier_semaphore()
    for p in peers:
        pl.semaphore_signal(barrier, inc=1, device_id=(b, p), device_id_type=MESH)
    for i in range(1, STEPS):
        pl.semaphore_signal(barrier, inc=1, device_id=(later[i], u), device_id_type=MESH)
        pl.semaphore_signal(barrier, inc=1, device_id=(earlier[i], u), device_id_type=MESH)

    def cols(index, size):
        return pl.ds(pl.multiple_of(index * size, size), size)

    locals_ = [
        pltpu.make_async_copy(q_hbm, q, local_sem.at[0]),
        pltpu.make_async_copy(k_hbm, k.at[0], local_sem.at[1]),
        pltpu.make_async_copy(lse_hbm, lse, local_sem.at[2]),
        pltpu.make_async_copy(v_hbm, v.at[0], local_sem.at[3]),
        pltpu.make_async_copy(o_hbm, o, local_sem.at[4]),
        pltpu.make_async_copy(g_hbm.at[:, cols(u, width)], g.at[cols(u, piece), :], local_sem.at[5]),
    ]
    for c in locals_:
        c.start()
    pl.semaphore_wait(barrier, len(peers) + 2 * (STEPS - 1))

    def remote(src, dst, send, recv, to):
        return pltpu.make_async_remote_copy(
            src_ref=src, dst_ref=dst, send_sem=send, recv_sem=recv, device_id=to, device_id_type=MESH
        )

    g_copies = [
        remote(g_hbm.at[:, cols(p, width)], g.at[cols(u, piece), :], g_send.at[n], g_recv.at[n], (b, p))
        for n, p in enumerate(peers)
    ]
    kv_copies = []
    for i in range(1, STEPS):
        kv_copies.append(remote(k_hbm, k.at[i], kv_send.at[0, i - 1], kv_recv.at[0, i - 1], (later[i], u)))
        kv_copies.append(remote(v_hbm, v.at[i], kv_send.at[1, i - 1], kv_recv.at[1, i - 1], (later[i], u)))
    for c in g_copies[:2]:
        c.start()
    for c in kv_copies[0::2]:
        c.start()
    for c in g_copies[2:]:
        c.start()
    for c in kv_copies[1::2]:
        c.start()

    def head(r):
        return slice(r * HEAD_DIM, (r + 1) * HEAD_DIM)

    for c in locals_[:3]:
        c.wait()
    for i in range(STEPS):
        if i:
            kv_copies[2 * (i - 1)].wait_recv()
        keys = k[i]
        kt[:, head(i)] = keys.T
        for r in range(group):
            s = dot_nt(keys, q[:, head(r)])
            p = jnp.exp(s * scale - lse[r : r + 1, :])
            prob[i, :, head(r)] = p
            prob_low[i, :, head(r)] = p.astype(BF16)

    for c in locals_[3:]:
        c.wait()
    for c in g_copies:
        c.wait_recv()

    grads = jnp.concatenate([g[:, head(r)] for r in range(group)], axis=0)
    queries = jnp.concatenate([q[:, head(r)] for r in range(group)], axis=0)
    part_copies = []

    def send_part(kind, i):
        c = remote(
            part.at[kind, i - 1], far.at[kind, i - 1], p_send.at[kind, i - 1], p_recv.at[kind, i - 1],
            (earlier[i], u),
        )
        c.start()
        part_copies.append(c)

    for i in (2, 1, 0):
        dv = dot_nn(prob_low[i], grads)
        if i:
            part[1, i - 1] = dv.astype(BF16)
            send_part(1, i)
        else:
            own[1] = dv

    ones = jnp.ones((8, HEAD_DIM), BF16)
    for r in range(group):
        product = g[:, head(r)].astype(F32) * o[:, head(r)].astype(F32)
        high = product.astype(BF16)
        low = (product - high.astype(F32)).astype(BF16)
        delta[:, head(r)] = dot_nt(ones, high) + dot_nt(ones, low)

    for c in kv_copies[1::2]:
        c.wait_recv()
    for i in (2, 1, 0):
        for r in range(group):
            dp = dot_nt(v[i], g[:, head(r)])
            ds = prob[i, :, head(r)] * (dp - delta[0:1, head(r)])
            dscore[head(i), head(r)] = ds.astype(BF16)
        dk = dot_nn(dscore[head(i), :], queries)
        if i:
            part[0, i - 1] = dk.astype(BF16)
            send_part(0, i)
        else:
            own[0] = dk

    for r in range(group):
        dqt = dot_nn(kt[...], dscore[:, head(r)])
        dq[:, head(r)] = (dqt.T * scale).astype(BF16)

    dq_copies = []
    for n, p in enumerate(peers):
        c = remote(dq.at[cols(p, piece), :], dq_out.at[:, cols(u, width)], dq_send.at[n], dq_recv.at[n], (b, p))
        c.start()
        dq_copies.append(c)
    keep = [pltpu.make_async_copy(dq.at[cols(u, piece), :], dq_out.at[:, cols(u, width)], local_out_sem.at[0])]
    keep[0].start()

    for c in part_copies:
        c.wait_recv()
    final_copies = []
    for kind, out, factor in ((1, dv_out, None), (0, dk_out, scale)):
        total = own[kind] + far[kind, 0].astype(F32) + far[kind, 1].astype(F32)
        if factor is not None:
            total = total * factor
        final[kind] = total.astype(BF16)
        for n, p in enumerate(peers):
            c = remote(
                final.at[kind, cols(p, piece), :], out.at[:, cols(u, HEAD_DIM)],
                f_send.at[kind, n], f_recv.at[kind, n], (b, p),
            )
            c.start()
            final_copies.append(c)
        c = pltpu.make_async_copy(
            final.at[kind, cols(u, piece), :], out.at[:, cols(u, HEAD_DIM)], local_out_sem.at[1 + kind]
        )
        c.start()
        keep.append(c)

    for c in g_copies + kv_copies + part_copies:
        c.wait_send()
    for c in keep:
        c.wait()
    for c in dq_copies + final_copies:
        c.wait()


def solution(mesh):
    blocks = mesh.shape["blk"]
    ulys = mesh.shape["uly"]

    def body(q, k, v, o, g, lse):
        tokens, width = q.shape
        group = width // HEAD_DIM
        piece = tokens // ulys
        peers = len(HOPS)
        far = STEPS - 1
        dma = pltpu.SemaphoreType.DMA
        return pl.pallas_call(
            lambda *refs: kernel(blocks, ulys, *refs),
            out_shape=(
                jax.ShapeDtypeStruct((piece, width * ulys), BF16),
                jax.ShapeDtypeStruct((piece, HEAD_DIM * ulys), BF16),
                jax.ShapeDtypeStruct((piece, HEAD_DIM * ulys), BF16),
            ),
            in_specs=[pl.BlockSpec(memory_space=pl.ANY)] * 6,
            out_specs=(pl.BlockSpec(memory_space=pl.ANY),) * 3,
            scratch_shapes=[
                pltpu.VMEM((tokens, width), BF16),
                pltpu.VMEM((STEPS, tokens, HEAD_DIM), BF16),
                pltpu.VMEM((STEPS, tokens, HEAD_DIM), BF16),
                pltpu.VMEM((tokens, width), BF16),
                pltpu.VMEM((tokens, width), BF16),
                pltpu.VMEM((group, tokens), F32),
                pltpu.VMEM((HEAD_DIM, STEPS * tokens), BF16),
                pltpu.VMEM((STEPS, tokens, width), F32),
                pltpu.VMEM((STEPS, tokens, width), BF16),
                pltpu.VMEM((STEPS * tokens, width), BF16),
                pltpu.VMEM((8, width), F32),
                pltpu.VMEM((2, tokens, HEAD_DIM), F32),
                pltpu.VMEM((2, far, tokens, HEAD_DIM), BF16),
                pltpu.VMEM((2, far, tokens, HEAD_DIM), BF16),
                pltpu.VMEM((tokens, width), BF16),
                pltpu.VMEM((2, tokens, HEAD_DIM), BF16),
                dma((6,)),
                dma((3,)),
                dma((peers,)),
                dma((peers,)),
                dma((2, far)),
                dma((2, far)),
                dma((2, far)),
                dma((2, far)),
                dma((peers,)),
                dma((peers,)),
                dma((2, peers)),
                dma((2, peers)),
            ],
            compiler_params=pltpu.CompilerParams(collective_id=0, has_side_effects=True),
            name="grads",
        )(q, k, v, o, g, lse)

    placed = (
        P("blk", "uly"),
        P("blk", "uly"),
        P("blk", "uly"),
        P("blk", "uly"),
        P(("blk", "uly"), None),
        P("uly", "blk"),
    )
    return jax.shard_map(
        body,
        mesh=mesh,
        in_specs=placed,
        out_specs=(P(("blk", "uly"), None), P(("blk", "uly"), None), P(("blk", "uly"), None)),
        check_vma=False,
    )
```

time: 114 us -> 47.2 us (0.41)
  starting transfers between devices: 64.9 us -> 0 us
  Pallas kernels: 0 us -> 43.3 us
  waiting for transfers between devices: 36.2 us -> 0 us
  matrix products: 4.34 us -> 0 us
  local copies, waits for them, and re-layouts: 6.55 us -> 2.99 us
    pallas_call x0 -> x1, Pallas kernels: none -> 43.3 us  [body(): pl.pallas_call(lambda *refs: kernel(blocks, ulys, *refs), out_shape=(jax....]
    all_to_all x4 -> x0, waiting for transfers between devices: 35 us -> none  [the longest x1 9.4 us: body(): lax.all_to_all(query_low, 'uly', split_axis=0, concat_axis=1, tiled=True)]
    ppermute x8 -> x0, starting transfers between devices: 33.2 us -> none  [shifted(): lax.ppermute(array, axis, [(i, (i + by) % size) for i in range(size)])]
    all_to_all x4 -> x0, starting transfers between devices: 31.7 us -> none  [the longest x1 16.2 us: body(): lax.all_to_all(output_grad, 'uly', split_axis=1, concat_axis=0, tiled=True)]
    all_to_all x5 -> x0, local copies, waits for them, and re-layouts: 4.38 us -> none  [the longest x1 1.6 us: body(): lax.all_to_all(output_grad, 'uly', split_axis=1, concat_axis=0, tiled=True)]
    dot_general x15 -> x0, matrix products: 4.34 us -> none  [the longest x3 1.23 us: block_grads(): jnp.einsum('grtu,tgrd->ugd', grad_scores, query_heads, preferred_element_...]
    ppermute x8 -> x0, waiting for transfers between devices: 1.22 us -> none  [shifted(): lax.ppermute(array, axis, [(i, (i + by) % size) for i in range(size)])]
    unnamed x13 -> x7, local copies, waits for them, and re-layouts: 1.82 us -> 2.99 us
  transfers between devices with their start and end apart: 12 -> 0, of which waited for: 5 -> 0; matrix products, arithmetic and copies ran while one was open for 7% -> 0% of each run, Pallas kernels for 0% -> 0%
where the time goes in v1:
time: 47.2 us; the launch traced here: 47 us
  Pallas kernels  43.3 us (92%)
  local copies, waits for them, and re-layouts  2.99 us (6%)
  between operations  0.65 us (1%)
    pallas_call x1, Pallas kernels, body(): pl.pallas_call(lambda *refs: kernel(blocks, ulys, *refs), out_shape=(jax....  43.3 us
    unnamed x7, local copies, waits for them, and re-layouts  2.99 us

profile of v1, /device:TPU:1, one launch (start us, length us, event | category | flops | bytes accessed | tf_op | source)
XLA Modules:
  0.0 47.0 jit_solution(13227224784052122057)
XLA Ops:
  0.6 43.3 %grads.1 = (bf16[16,5120]{1,0:T(8,128)(2,1)}, bf16[16,1024]{1,0:T(8,128)(2,1)}, bf16[16,1024]{1,0:T(8,128)(2,1)}) custom-call(bf16[128,640]{1,0:T(8,128)(2,1)} %refs_0_.1, bf16[128,128]{1,0:T(8,128)(2,1)} %refs_1_.1, bf16[128,128]{1,0:T(8,128)(2,1)} %refs_2_.1, bf16[128,640]{1,0:T(8,128)(2,1)} %refs_3_.1, bf16[16,5120]{1,0:T(8,128)(2,1)} %refs_4_.1, ...), custom_call_target="tpu_custom_call" | custom-call | tf_op jit(solution)/shard_map/grads/pallas_call | solution.py:211
  44.0 0.0 copy-start.1
  44.0 1.6 %copy.12 = bf16[16,5120]{1,0:T(8,128)(2,1)} copy(bf16[16,5120]{1,0:T(8,128)(2,1)} %get-tuple-element.6) | data formatting | bytes 327680
  45.6 0.0 copy-done.1
  45.6 0.0 copy-start
  45.6 0.6 %copy.13 = bf16[16,1024]{1,0:T(8,128)(2,1)} copy(bf16[16,1024]{1,0:T(8,128)(2,1)S(1)} %copy-done.1) | data formatting | bytes 65536
  46.2 0.2 copy-done
  46.3 0.6 %copy.14 = bf16[16,1024]{1,0:T(8,128)(2,1)} copy(bf16[16,1024]{1,0:T(8,128)(2,1)S(1)} %copy-done) | data formatting | bytes 65536
Async XLA Ops:
  44.0 1.6 %copy-start.1 = (bf16[16,1024]{1,0:T(8,128)(2,1)S(1)}, bf16[16,1024]{1,0:T(8,128)(2,1)}, u32[]{:S(2)}) copy-start(bf16[16,1024]{1,0:T(8,128)(2,1)} %get-tuple-element.7) | copy-start | bytes 98308
  45.6 0.8 %copy-start = (bf16[16,1024]{1,0:T(8,128)(2,1)S(1)}, bf16[16,1024]{1,0:T(8,128)(2,1)}, u32[]{:S(2)}) copy-start(bf16[16,1024]{1,0:T(8,128)(2,1)} %get-tuple-element.8) | copy-start | bytes 98308

commit v2 on v1

--- a/solution.py
+++ b/solution.py
@@ -197,6 +197,17 @@
         c.wait()
 
 
+def put_out(a, b, c, a_out, b_out, c_out, sem):
+    copies = [
+        pltpu.make_async_copy(src, dst, sem.at[n])
+        for n, (src, dst) in enumerate(((a, a_out), (b, b_out), (c, c_out)))
+    ]
+    for copy in copies:
+        copy.start()
+    for copy in copies:
+        copy.wait()
+
+
 def solution(mesh):
     blocks = mesh.shape["blk"]
     ulys = mesh.shape["uly"]
@@ -208,12 +219,12 @@
         peers = len(HOPS)
         far = STEPS - 1
         dma = pltpu.SemaphoreType.DMA
-        return pl.pallas_call(
+        held = pl.pallas_call(
             lambda *refs: kernel(blocks, ulys, *refs),
             out_shape=(
-                jax.ShapeDtypeStruct((piece, width * ulys), BF16),
-                jax.ShapeDtypeStruct((piece, HEAD_DIM * ulys), BF16),
-                jax.ShapeDtypeStruct((piece, HEAD_DIM * ulys), BF16),
+                pltpu.VMEM((piece, width * ulys), BF16),
+                pltpu.VMEM((piece, HEAD_DIM * ulys), BF16),
+                pltpu.VMEM((piece, HEAD_DIM * ulys), BF16),
             ),
             in_specs=[pl.BlockSpec(memory_space=pl.ANY)] * 6,
             out_specs=(pl.BlockSpec(memory_space=pl.ANY),) * 3,
@@ -250,6 +261,15 @@
             compiler_params=pltpu.CompilerParams(collective_id=0, has_side_effects=True),
             name="grads",
         )(q, k, v, o, g, lse)
+        return pl.pallas_call(
+            put_out,
+            out_shape=tuple(jax.ShapeDtypeStruct(x.shape, x.dtype) for x in held),
+            in_specs=[pl.BlockSpec(memory_space=pl.ANY)] * 3,
+            out_specs=(pl.BlockSpec(memory_space=pl.ANY),) * 3,
+            scratch_shapes=[dma((3,))],
+            compiler_params=pltpu.CompilerParams(vmem_limit_bytes=2**20),
+            name="put_out",
+        )(*held)
 
     placed = (
         P("blk", "uly"),

time: 47.2 us -> 44.7 us (0.947)
  local copies, waits for them, and re-layouts: 2.99 us -> 0 us
  Pallas kernels: 43.3 us -> 43.9 us
    unnamed x7 -> x0, local copies, waits for them, and re-layouts: 2.99 us -> none
    pallas_call x1 -> x2, Pallas kernels: 43.3 us -> 43.9 us  [the longest x1 43.2 us: body(): pl.pallas_call(lambda *refs: kernel(blocks, ulys, *refs), out_shape=(pltp...]
where the time goes in v2:
time: 44.7 us; the launch traced here: 44.5 us
  Pallas kernels  43.9 us (98%)
  between operations  0.64 us (1%)
    pallas_call x1, Pallas kernels, body(): pl.pallas_call(lambda *refs: kernel(blocks, ulys, *refs), out_shape=(pltp...  43.2 us

profile of v2, /device:TPU:1, one launch (start us, length us, event | category | flops | bytes accessed | tf_op | source)
XLA Modules:
  0.0 44.5 jit_solution(4308801464365082304)
XLA Ops:
  0.6 43.2 %grads.1 = (bf16[16,5120]{1,0:T(8,128)(2,1)S(1)}, bf16[16,1024]{1,0:T(8,128)(2,1)S(1)}, bf16[16,1024]{1,0:T(8,128)(2,1)S(1)}) custom-call(bf16[128,640]{1,0:T(8,128)(2,1)} %refs_0_.1, bf16[128,128]{1,0:T(8,128)(2,1)} %refs_1_.1, bf16[128,128]{1,0:T(8,128)(2,1)} %refs_2_.1, bf16[128,640]{1,0:T(8,128)(2,1)} %refs_3_.1, bf16[16,5120]{1,0:T(8,128)(2,1)} %refs_4_.1, ...), custom_call_target="tpu_custom_call" | custom-call | tf_op jit(solution)/shard_map/grads/pallas_call | solution.py:222
  43.8 0.7 %put_out.1 = (bf16[16,5120]{1,0:T(8,128)(2,1)}, bf16[16,1024]{1,0:T(8,128)(2,1)}, bf16[16,1024]{1,0:T(8,128)(2,1)}) custom-call(bf16[16,5120]{1,0:T(8,128)(2,1)S(1)} %get-tuple-element.6.a, bf16[16,1024]{1,0:T(8,128)(2,1)S(1)} %get-tuple-element.7.b, bf16[16,1024]{1,0:T(8,128)(2,1)S(1)} %get-tuple-element.8.c), custom_call_target="tpu_custom_call" | custom-call | tf_op jit(solution)/shard_map/put_out/pallas_call | solution.py:264

commit v3 on v2

--- a/solution.py
+++ b/solution.py
@@ -14,6 +14,9 @@
 BF16 = jnp.bfloat16
 
 HOPS = ((2, 0), (2, 1), (1, 0), (3, 0), (1, 1), (3, 1), (0, 1))
+INVERSE = (0, 1, 3, 2, 5, 4, 6)
+FIRST = (0, 1, 2, 4, 3, 5, 6)
+LAST = (6, 2, 4, 0, 1, 3, 5)
 
 
 def dot_nt(a, b):
@@ -30,7 +33,7 @@
     dq_out, dk_out, dv_out,
     q, k, v, o, g, lse, kt, prob, prob_low, dscore, delta, own, part, far, dq, final,
     local_sem, local_out_sem, g_send, g_recv, kv_send, kv_recv, p_send, p_recv,
-    dq_send, dq_recv, f_send, f_recv,
+    dq_send, dq_recv, f_send, f_recv, go_uly, go_blk,
 ):
     group = q.shape[1] // HEAD_DIM
     tokens = q.shape[0]
@@ -50,12 +53,30 @@
     later = [(b + i) % blocks for i in range(STEPS)]
     earlier = [(b + blocks - i) % blocks for i in range(STEPS)]
 
+    def zero(index, size):
+        return 1 - (index + size - 1) // size
+
+    def turn(to):
+        return 2 * to + (ulys - 1) * zero(b, blocks) * zero(to, ulys)
+
+    def place(block):
+        return block % 3 + 3 * zero(block, blocks) * zero(u, ulys)
+
+    now, mine = turn(u), place(b)
+    others = [(turn(p), now) for p in peers] + [(place(x), mine) for x in later[1:] + earlier[1:]]
+    before = sum((their < own_).astype(jnp.int32) for their, own_ in others)
     barrier = pltpu.get_barrier_semaphore()
-    for p in peers:
-        pl.semaphore_signal(barrier, inc=1, device_id=(b, p), device_id_type=MESH)
-    for i in range(1, STEPS):
-        pl.semaphore_signal(barrier, inc=1, device_id=(later[i], u), device_id_type=MESH)
-        pl.semaphore_signal(barrier, inc=1, device_id=(earlier[i], u), device_id_type=MESH)
+
+    def tell(sem, index, to, when):
+        @pl.when(when)
+        def _():
+            pl.semaphore_signal(sem if index is None else sem.at[index], inc=1, device_id=to, device_id_type=MESH)
+
+    for n in FIRST:
+        tell(barrier, None, (b, peers[n]), turn(peers[n]) > now)
+    for i in range(1, STEPS):
+        for other in (later[i], earlier[i]):
+            tell(barrier, None, (other, u), place(other) > mine)
 
     def cols(index, size):
         return pl.ds(pl.multiple_of(index * size, size), size)
@@ -70,7 +91,20 @@
     ]
     for c in locals_:
         c.start()
-    pl.semaphore_wait(barrier, len(peers) + 2 * (STEPS - 1))
+    @pl.when(before > 0)
+    def _():
+        pl.semaphore_wait(barrier, before)
+
+    for n in FIRST:
+        tell(go_uly, INVERSE[n], (b, peers[n]), turn(peers[n]) < now)
+    for i in range(1, STEPS):
+        tell(go_blk, i - 1, (earlier[i], u), place(earlier[i]) < mine)
+        tell(go_blk, STEPS - 2 + i, (later[i], u), place(later[i]) < mine)
+
+    def await_go(sem, index, when):
+        @pl.when(when)
+        def _():
+            pl.semaphore_wait(sem.at[index], 1)
 
     def remote(src, dst, send, recv, to):
         return pltpu.make_async_remote_copy(
@@ -85,14 +119,27 @@
     for i in range(1, STEPS):
         kv_copies.append(remote(k_hbm, k.at[i], kv_send.at[0, i - 1], kv_recv.at[0, i - 1], (later[i], u)))
         kv_copies.append(remote(v_hbm, v.at[i], kv_send.at[1, i - 1], kv_recv.at[1, i - 1], (later[i], u)))
-    for c in g_copies[:2]:
-        c.start()
-    for c in kv_copies[0::2]:
-        c.start()
-    for c in g_copies[2:]:
-        c.start()
-    for c in kv_copies[1::2]:
-        c.start()
+    def send_g(n, when):
+        @pl.when(when)
+        def _():
+            g_copies[n].start()
+
+    for i in range(1, STEPS):
+        for c in kv_copies[2 * (i - 1) : 2 * i]:
+            @pl.when(place(later[i]) < mine)
+            def _():
+                c.start()
+    for n in FIRST:
+        send_g(n, turn(peers[n]) < now)
+    for i in range(1, STEPS):
+        await_go(go_blk, i - 1, place(later[i]) > mine)
+        for c in kv_copies[2 * (i - 1) : 2 * i]:
+            @pl.when(place(later[i]) > mine)
+            def _():
+                c.start()
+    for n in LAST:
+        await_go(go_uly, n, turn(peers[n]) > now)
+        send_g(n, turn(peers[n]) > now)
 
     def head(r):
         return slice(r * HEAD_DIM, (r + 1) * HEAD_DIM)
@@ -127,6 +174,8 @@
         c.start()
         part_copies.append(c)
 
+    for i in range(1, STEPS):
+        await_go(go_blk, STEPS - 2 + i, place(earlier[i]) > mine)
     for i in (2, 1, 0):
         dv = dot_nn(prob_low[i], grads)
         if i:
@@ -168,10 +217,10 @@
     keep = [pltpu.make_async_copy(dq.at[cols(u, piece), :], dq_out.at[:, cols(u, width)], local_out_sem.at[0])]
     keep[0].start()
 
-    for c in part_copies:
-        c.wait_recv()
     final_copies = []
     for kind, out, factor in ((1, dv_out, None), (0, dk_out, scale)):
+        for c in part_copies[2 * (1 - kind) : 2 * (2 - kind)]:
+            c.wait_recv()
         total = own[kind] + far[kind, 0].astype(F32) + far[kind, 1].astype(F32)
         if factor is not None:
             total = total * factor
@@ -257,6 +306,8 @@
                 dma((peers,)),
                 dma((2, peers)),
                 dma((2, peers)),
+                pltpu.SemaphoreType.REGULAR((peers,)),
+                pltpu.SemaphoreType.REGULAR((2 * far,)),
             ],
             compiler_params=pltpu.CompilerParams(collective_id=0, has_side_effects=True),
             name="grads",

time: 44.7 us -> 43.2 us (0.966)
  Pallas kernels: 43.9 us -> 42.4 us
    pallas_call x1, Pallas kernels: 43.2 us -> 41.7 us  [body(): pl.pallas_call(lambda *refs: kernel(blocks, ulys, *refs), out_shape=(pltp...]
where the time goes in v3:
time: 43.2 us; the launch traced here: 43 us
  Pallas kernels  42.4 us (98%)
  between operations  0.64 us (1%)
    pallas_call x1, Pallas kernels, body(): pl.pallas_call(lambda *refs: kernel(blocks, ulys, *refs), out_shape=(pltp...  41.7 us

profile of v3, /device:TPU:1, one launch (start us, length us, event | category | flops | bytes accessed | tf_op | source)
XLA Modules:
  0.0 43.0 jit_solution(13622789511946576963)
XLA Ops:
  0.6 41.7 %grads.1 = (bf16[16,5120]{1,0:T(8,128)(2,1)S(1)}, bf16[16,1024]{1,0:T(8,128)(2,1)S(1)}, bf16[16,1024]{1,0:T(8,128)(2,1)S(1)}) custom-call(bf16[128,640]{1,0:T(8,128)(2,1)} %refs_0_.1, bf16[128,128]{1,0:T(8,128)(2,1)} %refs_1_.1, bf16[128,128]{1,0:T(8,128)(2,1)} %refs_2_.1, bf16[128,640]{1,0:T(8,128)(2,1)} %refs_3_.1, bf16[16,5120]{1,0:T(8,128)(2,1)} %refs_4_.1, ...), custom_call_target="tpu_custom_call" | custom-call | tf_op jit(solution)/shard_map/grads/pallas_call | solution.py:271
  42.3 0.7 %put_out.1 = (bf16[16,5120]{1,0:T(8,128)(2,1)}, bf16[16,1024]{1,0:T(8,128)(2,1)}, bf16[16,1024]{1,0:T(8,128)(2,1)}) custom-call(bf16[16,5120]{1,0:T(8,128)(2,1)S(1)} %get-tuple-element.6.a, bf16[16,1024]{1,0:T(8,128)(2,1)S(1)} %get-tuple-element.7.b, bf16[16,1024]{1,0:T(8,128)(2,1)S(1)} %get-tuple-element.8.c), custom_call_target="tpu_custom_call" | custom-call | tf_op jit(solution)/shard_map/put_out/pallas_call | solution.py:315

commit v4 on v3

--- a/solution.py
+++ b/solution.py
@@ -15,8 +15,11 @@
 
 HOPS = ((2, 0), (2, 1), (1, 0), (3, 0), (1, 1), (3, 1), (0, 1))
 INVERSE = (0, 1, 3, 2, 5, 4, 6)
+SOONER = (0,)
+FINALS = (0, 1, 2, 3)
 FIRST = (0, 1, 2, 4, 3, 5, 6)
-LAST = (6, 2, 4, 0, 1, 3, 5)
+NEAR = (5, 6, 0, 1, 2, 3, 4)
+LAST = (2, 4, 0, 1, 3, 5, 6)
 
 
 def dot_nt(a, b):
@@ -33,7 +36,7 @@
     dq_out, dk_out, dv_out,
     q, k, v, o, g, lse, kt, prob, prob_low, dscore, delta, own, part, far, dq, final,
     local_sem, local_out_sem, g_send, g_recv, kv_send, kv_recv, p_send, p_recv,
-    dq_send, dq_recv, f_send, f_recv, go_uly, go_blk,
+    dq_send, dq_recv, f_send, f_recv, go_uly, go_blk, g_all,
 ):
     group = q.shape[1] // HEAD_DIM
     tokens = q.shape[0]
@@ -89,6 +92,8 @@
         pltpu.make_async_copy(o_hbm, o, local_sem.at[4]),
         pltpu.make_async_copy(g_hbm.at[:, cols(u, width)], g.at[cols(u, piece), :], local_sem.at[5]),
     ]
+    slab = pltpu.make_async_copy(g_hbm, g_all, local_sem.at[6])
+    slab.start()
     for c in locals_:
         c.start()
     @pl.when(before > 0)
@@ -112,7 +117,7 @@
         )
 
     g_copies = [
-        remote(g_hbm.at[:, cols(p, width)], g.at[cols(u, piece), :], g_send.at[n], g_recv.at[n], (b, p))
+        remote(g_all.at[:, cols(p, width)], g.at[cols(u, piece), :], g_send.at[n], g_recv.at[n], (b, p))
         for n, p in enumerate(peers)
     ]
     kv_copies = []
@@ -129,6 +134,7 @@
             @pl.when(place(later[i]) < mine)
             def _():
                 c.start()
+    slab.wait()
     for n in FIRST:
         send_g(n, turn(peers[n]) < now)
     for i in range(1, STEPS):
@@ -176,13 +182,12 @@
 
     for i in range(1, STEPS):
         await_go(go_blk, STEPS - 2 + i, place(earlier[i]) > mine)
-    for i in (2, 1, 0):
-        dv = dot_nn(prob_low[i], grads)
-        if i:
-            part[1, i - 1] = dv.astype(BF16)
-            send_part(1, i)
-        else:
-            own[1] = dv
+    rows = STEPS * tokens
+    dv = dot_nn(prob_low[...].reshape(rows, width), grads)
+    for i in (2, 1):
+        part[1, i - 1] = dv[head(i)].astype(BF16)
+        send_part(1, i)
+    own[1] = dv[head(0)]
 
     ones = jnp.ones((8, HEAD_DIM), BF16)
     for r in range(group):
@@ -193,31 +198,46 @@
 
     for c in kv_copies[1::2]:
         c.wait_recv()
-    for i in (2, 1, 0):
-        for r in range(group):
-            dp = dot_nt(v[i], g[:, head(r)])
-            ds = prob[i, :, head(r)] * (dp - delta[0:1, head(r)])
-            dscore[head(i), head(r)] = ds.astype(BF16)
-        dk = dot_nn(dscore[head(i), :], queries)
-        if i:
-            part[0, i - 1] = dk.astype(BF16)
-            send_part(0, i)
-        else:
-            own[0] = dk
+    values = v[...].reshape(rows, HEAD_DIM)
+    for r in range(group):
+        dp = dot_nt(values, g[:, head(r)])
+        ds = prob[:, :, head(r)].reshape(rows, HEAD_DIM) * (dp - delta[0:1, head(r)])
+        dscore[:, head(r)] = ds.astype(BF16)
+    dk = dot_nn(dscore[...], queries)
+    for i in (2, 1):
+        part[0, i - 1] = dk[head(i)].astype(BF16)
+        send_part(0, i)
+    own[0] = dk[head(0)]
 
     for r in range(group):
         dqt = dot_nn(kt[...], dscore[:, head(r)])
-        dq[:, head(r)] = (dqt.T * scale).astype(BF16)
-
-    dq_copies = []
-    for n, p in enumerate(peers):
-        c = remote(dq.at[cols(p, piece), :], dq_out.at[:, cols(u, width)], dq_send.at[n], dq_recv.at[n], (b, p))
-        c.start()
-        dq_copies.append(c)
+        dq[:, head(r)] = (dqt * scale).astype(BF16).T
+
+    dq_copies = [
+        remote(dq.at[cols(p, piece), :], dq_out.at[:, cols(u, width)], dq_send.at[n], dq_recv.at[n], (b, p))
+        for n, p in enumerate(peers)
+    ]
+    final_copies = [
+        [
+            remote(
+                final.at[kind, cols(p, piece), :], out.at[:, cols(u, HEAD_DIM)],
+                f_send.at[kind, n], f_recv.at[kind, n], (b, p),
+            )
+            for n, p in enumerate(peers)
+        ]
+        for kind, out in ((0, dk_out), (1, dv_out))
+    ]
+
+    def start_some(copies, chips_):
+        for n, p in enumerate(peers):
+            @pl.when(sum((p // 2 == chip).astype(jnp.int32) for chip in chips_) > 0)
+            def _():
+                copies[n].start()
+
+    start_some(dq_copies, SOONER)
     keep = [pltpu.make_async_copy(dq.at[cols(u, piece), :], dq_out.at[:, cols(u, width)], local_out_sem.at[0])]
     keep[0].start()
 
-    final_copies = []
     for kind, out, factor in ((1, dv_out, None), (0, dk_out, scale)):
         for c in part_copies[2 * (1 - kind) : 2 * (2 - kind)]:
             c.wait_recv()
@@ -225,18 +245,19 @@
         if factor is not None:
             total = total * factor
         final[kind] = total.astype(BF16)
-        for n, p in enumerate(peers):
-            c = remote(
-                final.at[kind, cols(p, piece), :], out.at[:, cols(u, HEAD_DIM)],
-                f_send.at[kind, n], f_recv.at[kind, n], (b, p),
-            )
-            c.start()
-            final_copies.append(c)
+        start_some(final_copies[kind], FINALS)
         c = pltpu.make_async_copy(
             final.at[kind, cols(u, piece), :], out.at[:, cols(u, HEAD_DIM)], local_out_sem.at[1 + kind]
         )
         c.start()
         keep.append(c)
+    for chip in range(chips):
+        if chip not in SOONER:
+            start_some(dq_copies, (chip,))
+        if chip not in FINALS:
+            start_some(final_copies[1], (chip,))
+            start_some(final_copies[0], (chip,))
+    final_copies = final_copies[0] + final_copies[1]
 
     for c in g_copies + kv_copies + part_copies:
         c.wait_send()
@@ -294,7 +315,7 @@
                 pltpu.VMEM((2, far, tokens, HEAD_DIM), BF16),
                 pltpu.VMEM((tokens, width), BF16),
                 pltpu.VMEM((2, tokens, HEAD_DIM), BF16),
-                dma((6,)),
+                dma((7,)),
                 dma((3,)),
                 dma((peers,)),
                 dma((peers,)),
@@ -308,6 +329,7 @@
                 dma((2, peers)),
                 pltpu.SemaphoreType.REGULAR((peers,)),
                 pltpu.SemaphoreType.REGULAR((2 * far,)),
+                pltpu.VMEM((piece, width * ulys), BF16),
             ],
             compiler_params=pltpu.CompilerParams(collective_id=0, has_side_effects=True),
             name="grads",

time: 43.2 us -> 41.5 us (0.961)
  the two profiles are of different devices: /device:TPU:1 before, /device:TPU:91 now
where the time goes in v4:
time: 41.5 us; the launch traced here: 41.4 us
  Pallas kernels  40.7 us (98%)
  between operations  0.64 us (2%)
    pallas_call x1, Pallas kernels, body(): pl.pallas_call(lambda *refs: kernel(blocks, ulys, *refs), out_shape=(pltp...  40 us

profile of v4, /device:TPU:91, one launch (start us, length us, event | category | flops | bytes accessed | tf_op | source)
XLA Modules:
  0.0 41.4 jit_solution(11857306372895113378)
XLA Ops:
  0.6 40.0 %grads.1 = (bf16[16,5120]{1,0:T(8,128)(2,1)S(1)}, bf16[16,1024]{1,0:T(8,128)(2,1)S(1)}, bf16[16,1024]{1,0:T(8,128)(2,1)S(1)}) custom-call(bf16[128,640]{1,0:T(8,128)(2,1)} %refs_0_.1, bf16[128,128]{1,0:T(8,128)(2,1)} %refs_1_.1, bf16[128,128]{1,0:T(8,128)(2,1)} %refs_2_.1, bf16[128,640]{1,0:T(8,128)(2,1)} %refs_3_.1, bf16[16,5120]{1,0:T(8,128)(2,1)} %refs_4_.1, ...), custom_call_target="tpu_custom_call" | custom-call | tf_op jit(solution)/shard_map/grads/pallas_call | solution.py:292
  40.6 0.7 %put_out.1 = (bf16[16,5120]{1,0:T(8,128)(2,1)}, bf16[16,1024]{1,0:T(8,128)(2,1)}, bf16[16,1024]{1,0:T(8,128)(2,1)}) custom-call(bf16[16,5120]{1,0:T(8,128)(2,1)S(1)} %get-tuple-element.6.a, bf16[16,1024]{1,0:T(8,128)(2,1)S(1)} %get-tuple-element.7.b, bf16[16,1024]{1,0:T(8,128)(2,1)S(1)} %get-tuple-element.8.c), custom_call_target="tpu_custom_call" | custom-call | tf_op jit(solution)/shard_map/put_out/pallas_call | solution.py:337

commit v5 on v4

--- a/solution.py
+++ b/solution.py
@@ -19,7 +19,7 @@
 FINALS = (0, 1, 2, 3)
 FIRST = (0, 1, 2, 4, 3, 5, 6)
 NEAR = (5, 6, 0, 1, 2, 3, 4)
-LAST = (2, 4, 0, 1, 3, 5, 6)
+LAST = (6, 2, 4, 0, 1, 3, 5)
 
 
 def dot_nt(a, b):

time: 41.5 us -> 41.5 us (level)
  no operation moved by 1% of the time
where the time goes in v5:
time: 41.5 us; the launch traced here: 41.4 us
  Pallas kernels  40.7 us (98%)
  between operations  0.64 us (2%)
    pallas_call x1, Pallas kernels, body(): pl.pallas_call(lambda *refs: kernel(blocks, ulys, *refs), out_shape=(pltp...  40 us

profile of v5, /device:TPU:91, one launch (start us, length us, event | category | flops | bytes accessed | tf_op | source)
XLA Modules:
  0.0 41.4 jit_solution(6308712773798319510)
XLA Ops:
  0.6 40.0 %grads.1 = (bf16[16,5120]{1,0:T(8,128)(2,1)S(1)}, bf16[16,1024]{1,0:T(8,128)(2,1)S(1)}, bf16[16,1024]{1,0:T(8,128)(2,1)S(1)}) custom-call(bf16[128,640]{1,0:T(8,128)(2,1)} %refs_0_.1, bf16[128,128]{1,0:T(8,128)(2,1)} %refs_1_.1, bf16[128,128]{1,0:T(8,128)(2,1)} %refs_2_.1, bf16[128,640]{1,0:T(8,128)(2,1)} %refs_3_.1, bf16[16,5120]{1,0:T(8,128)(2,1)} %refs_4_.1, ...), custom_call_target="tpu_custom_call" | custom-call | tf_op jit(solution)/shard_map/grads/pallas_call | solution.py:292
  40.6 0.7 %put_out.1 = (bf16[16,5120]{1,0:T(8,128)(2,1)}, bf16[16,1024]{1,0:T(8,128)(2,1)}, bf16[16,1024]{1,0:T(8,128)(2,1)}) custom-call(bf16[16,5120]{1,0:T(8,128)(2,1)S(1)} %get-tuple-element.6.a, bf16[16,1024]{1,0:T(8,128)(2,1)S(1)} %get-tuple-element.7.b, bf16[16,1024]{1,0:T(8,128)(2,1)S(1)} %get-tuple-element.8.c), custom_call_target="tpu_custom_call" | custom-call | tf_op jit(solution)/shard_map/put_out/pallas_call | solution.py:337
